TPU v7x, 32 devices: a whole 2x2x4 slice. The times are simulated.
32 devices in a mesh: band: 4 (over y, core), grid: 8 (over z, x).
Axes of the slice: x: 2, y: 2, z: 4, core: 2. Of those that a mesh axis runs over, the one named last changes fastest.
Arguments:
- orbitals: float32 [64, 16, 4096], P('band', 'grid'), may hold values from -6 to 6
- potential: float32 [16, 4096], P('grid'), may hold values from 0 to 2
Outputs:
- rotated: bfloat16 [64, 16, 4096], P('band', 'grid')
All inputs are finite; a program needn't handle non-finite values. Where the computation divides by a largest or mean magnitude, that divisor is 1e-20 or more.
Results may differ from a plain program's by a relative error of at most 0.001.
The roundings to bfloat16 on the way count: a program that leaves them out, or rounds other values in their place, can miss the bound.
Values may be sent and summed in bfloat16 or wider, within the bound.
A program may use at most 64 MiB of HBM per device.

v0:
```python
import jax
import jax.numpy as jnp
from jax import lax
from jax.sharding import PartitionSpec as P

NX = 64
DEGREE = 2
NS_ITERS = 2


def with_halo(block, sides, width):
    for axis, dim in sides:
        count = lax.axis_size(axis)
        forward = [(i, i + 1) for i in range(count - 1)]
        forward.append((count - 1, 0))
        backward = [(target, source) for source, target in forward]
        low = lax.ppermute(
            lax.slice_in_dim(block, block.shape[dim] - width, None, axis=dim), axis, forward
        )
        high = lax.ppermute(lax.slice_in_dim(block, 0, width, axis=dim), axis, backward)
        block = jnp.concatenate([low, block, high], axis=dim)
    return block


def apply_inner(extended, potential):
    inner = extended[:, 1:-1]
    count = inner.shape[0]
    planes = inner.shape[1]
    square = inner.reshape(count, planes, NX, NX)
    sideways = jnp.roll(square, 1, 2) + jnp.roll(square, -1, 2)
    sideways = sideways + jnp.roll(square, 1, 3) + jnp.roll(square, -1, 3)
    beside = extended[:, 2:] + extended[:, :-2] + sideways.reshape(inner.shape)
    return 0.5 * (6.0 * inner - beside) + potential[None] * inner


def local(orbitals, potential):
    previous = orbitals
    current = orbitals
    for degree_step in range(DEGREE):
        extended = with_halo(current, (("grid", 1),), 1)
        applied = apply_inner(extended, potential)
        if degree_step == 0:
            following = (applied - 5.0 * current) / 3.0
        else:
            following = 2.0 * (applied - 5.0 * current) / 3.0 - previous
        previous = current
        current = following
    count, zplanes, width = orbitals.shape
    filtered = current.astype(jnp.bfloat16).reshape(count, zplanes * width)
    pieces = lax.all_to_all(filtered, "band", split_axis=1, concat_axis=0, tiled=True)
    total_cells = pieces.shape[1] * lax.axis_size("band") * lax.axis_size("grid")
    partial_value = (
        lax.dot_general(
            pieces, pieces, (((1,), (1,)), ((), ())), preferred_element_type=jnp.float32
        )
        / total_cells
    )
    gram = lax.psum(partial_value, ("band", "grid"))
    scale = jnp.max(jnp.sum(jnp.abs(gram), axis=1))
    identity_mat = jnp.eye(gram.shape[0], dtype=jnp.float32)
    upper = gram / scale
    lower = identity_mat
    for sweep in range(NS_ITERS):
        factor = 1.5 * identity_mat - 0.5 * jnp.dot(lower, upper, precision=lax.Precision.HIGHEST)
        upper = jnp.dot(upper, factor, precision=lax.Precision.HIGHEST)
        lower = jnp.dot(factor, lower, precision=lax.Precision.HIGHEST)
    root = (lower / jnp.sqrt(scale)).astype(jnp.bfloat16)
    turned = lax.dot_general(
        root, pieces, (((0,), (0,)), ((), ())), preferred_element_type=jnp.float32
    )
    turned = turned.astype(jnp.bfloat16)
    returned = lax.all_to_all(turned, "band", split_axis=0, concat_axis=1, tiled=True)
    return returned.reshape(count, zplanes, width)


def solution(mesh):
    placed = (P("band", "grid", None), P("grid", None))
    return jax.shard_map(
        local, mesh=mesh, in_specs=placed, out_specs=P("band", "grid", None), check_vma=False
    )
```

profile of v0, /device:TPU:0, one launch (start us, length us, event | category | flops | bytes accessed | tf_op | source)
XLA Modules:
  0.0 102.4 jit_solution(3121627851999156750)
XLA Ops:
  0.0 1.9 %fusion.24 = (f32[16,1,4096]{2,1,0:T(1,128)S(1)}, f32[16,1,4096]{2,1,0:T(1,128)S(1)}) fusion(f32[16,2,4096]{2,1,0:T(2,128)} %param.2), kind=kLoop, calls=%fused_computation.42 | loop fusion | bytes 1048576 | tf_op jit(solution)/shard_map/slice | solution.py:20
  1.9 6.1 %collective-permute-start = (f32[16,1,4096]{2,1,0:T(1,128)S(1)}, f32[16,1,4096]{2,1,0:T(1,128)S(1)}, u32[]{:S(2)}, u32[]{:S(2)}) collective-permute-start(f32[16,1,4096]{2,1,0:T(1,128)S(1)} %get-tuple-element.25), channel_id=1, source_target_pairs={{1,0},{2,1},{3,2},{4,3},{5,4},{6,5},{7,6},{0,7},{9,8},{10,9},{11,1... | collective-permute-start | bytes 786440 | tf_op jit(solution)/shard_map/ppermute | solution.py:20
  7.9 0.6 reshape.35
  8.6 0.4 fusion.19
  8.9 0.4 fusion.20
  9.5 0.5 copy-done.1
  10.1 0.9 fusion.4
  11.0 0.5 add.58
  11.5 2.0 %collective-permute-done = f32[16,1,4096]{2,1,0:T(1,128)S(1)} collective-permute-done((f32[16,1,4096]{2,1,0:T(1,128)S(1)}, f32[16,1,4096]{2,1,0:T(1,128)S(1)}, u32[]{:S(2)}, u32[]{:S(2)}) %collective-permute-start) | collective-permute-done | bytes 262176 | tf_op jit(solution)/shard_map/ppermute | solution.py:20
  13.5 5.0 %collective-permute-done.1 = f32[16,1,4096]{2,1,0:T(1,128)} collective-permute-done((f32[16,1,4096]{2,1,0:T(1,128)S(1)}, f32[16,1,4096]{2,1,0:T(1,128)}, u32[]{:S(2)}, u32[]{:S(2)}) %collective-permute-start.1) | collective-permute-done | bytes 262176 | tf_op jit(solution)/shard_map/ppermute | solution.py:17
  18.5 2.4 %broadcast_multiply_fusion = (f32[16,2,4096]{2,1,0:T(2,128)S(1)}, f32[16,2,4096]{2,1,0:T(2,128)S(1)}) fusion(f32[16,2,4096]{2,1,0:T(2,128)S(1)} %copy-done, f32[2,4096]{1,0:T(2,128)S(1)} %copy-done.1, f32[16,2,4096]{2,1,0:T(2,128)S(1)} %add.58, f32[16,1,4096]{2,1,0:T(1,128)} %collective-permute-done.1, f32[16,1,4096]{2,1,0:T(1,128)S(1)} %collective-permute-done), kind=kLoop, calls=%fused_computation.26 | loop fusion | flops 1572864 | bytes 2654208 | tf_op jit(solution)/shard_map/div | solution.py:43
  21.0 0.6 reshape.36
  21.6 0.4 fusion.16
  22.0 0.2 fusion.17
  22.2 0.4 fusion.15
  22.5 1.3 %fusion.23 = (f32[16,1,4096]{2,1,0:T(1,128)}, f32[16,1,4096]{2,1,0:T(1,128)}) fusion(f32[16,2,4096]{2,1,0:T(2,128)S(1)} %get-tuple-element.5), kind=kLoop, calls=%fused_computation.41 | loop fusion | bytes 1048576 | tf_op jit(solution)/shard_map/slice | solution.py:20
  23.9 3.5 %collective-permute-start.2 = (f32[16,1,4096]{2,1,0:T(1,128)}, f32[16,1,4096]{2,1,0:T(1,128)S(1)}, u32[]{:S(2)}, u32[]{:S(2)}) collective-permute-start(f32[16,1,4096]{2,1,0:T(1,128)} %get-tuple-element.23), channel_id=1, source_target_pairs={{1,0},{2,1},{3,2},{4,3},{5,4},{6,5},{7,6},{0,7},{9,8},{10,9},{11,1... | collective-permute-start | bytes 786440 | tf_op jit(solution)/shard_map/ppermute | solution.py:20
  27.4 0.9 fusion.6
  28.2 0.5 add.65
  28.8 8.5 %collective-permute-done.2 = f32[16,1,4096]{2,1,0:T(1,128)S(1)} collective-permute-done((f32[16,1,4096]{2,1,0:T(1,128)}, f32[16,1,4096]{2,1,0:T(1,128)S(1)}, u32[]{:S(2)}, u32[]{:S(2)}) %collective-permute-start.2) | collective-permute-done | bytes 262176 | tf_op jit(solution)/shard_map/ppermute | solution.py:20
  37.2 0.3 collective-permute-done.3
  37.5 2.6 %subtract_convert_fusion = bf16[16,2,4096]{2,1,0:T(2,128)(2,1)S(1)} fusion(f32[16,2,4096]{2,1,0:T(2,128)S(1)} %copy-done, f32[16,2,4096]{2,1,0:T(2,128)S(1)} %get-tuple-element.6, f32[16,2,4096]{2,1,0:T(2,128)S(1)} %add.65, f32[16,2,4096]{2,1,0:T(2,128)S(1)} %get-tuple-element.5, f32[16,1,4096]{2,1,0:T(1,128)} %collective-permute-done.3, ...), kind=kLoop, calls=%fused_computation.24 | loop fusion | flops 1835008 | bytes 2916352 | tf_op jit(solution)/shard_map/convert_element_type | solution.py:49
  40.3 8.6 %all_to_all.35 = bf16[16,4,2048]{2,0,1:T(8,128)(2,1)S(1)} all-to-all(bf16[16,4,2048]{2,0,1:T(8,128)(2,1)S(1)} %copy.7), channel_id=1, replica_groups=mesh['band'=4,'grid'=8] {'band'}, dimensions={1} | all-to-all | bytes 524288 | tf_op jit(solution)/shard_map/all_to_all | solution.py:50
  48.9 0.2 convolution_multiply_fusion.2
  49.1 39.0 %psum.7 = f32[64,64]{1,0:T(8,128)S(1)} all-reduce(f32[64,64]{1,0:T(8,128)S(1)} %convolution_multiply_fusion.2), channel_id=1, replica_groups=mesh['band'=4,'grid'=8] {'band','grid'}, use_global_device_ids=true, to_apply=%region_0.1 | all-reduce | flops 4096 | bytes 32768 | tf_op jit(solution)/shard_map/psum | solution.py:58
  88.2 0.6 reduce_max.9
  88.8 0.8 fusion.1
  89.6 0.8 fusion.14
  91.6 0.2 convolution_convert_fusion
  91.9 9.4 %all_to_all.36 = bf16[4,16,2048]{2,1,0:T(8,128)(2,1)S(1)} all-to-all(bf16[4,16,2048]{2,1,0:T(8,128)(2,1)S(1)} %bitcast.21), channel_id=1, replica_groups=mesh['band'=4,'grid'=8] {'band'}, dimensions={0} | all-to-all | bytes 524288 | tf_op jit(solution)/shard_map/all_to_all | solution.py:72
  101.2 0.2 copy.8
  101.5 0.9 reshape.37
  (15 shorter events, 1.1 us)
Async XLA Ops:
  0.0 7.9 %copy-start = (f32[16,2,4096]{2,1,0:T(2,128)S(1)}, f32[16,2,4096]{2,1,0:T(2,128)}, u32[]{:S(2)}) copy-start(f32[16,2,4096]{2,1,0:T(2,128)} %param.2) | copy-start | bytes 1572868
  1.9 11.6 %collective-permute-start = (f32[16,1,4096]{2,1,0:T(1,128)S(1)}, f32[16,1,4096]{2,1,0:T(1,128)S(1)}, u32[]{:S(2)}, u32[]{:S(2)}) collective-permute-start(f32[16,1,4096]{2,1,0:T(1,128)S(1)} %get-tuple-element.25), channel_id=1, source_target_pairs={{1,0},{2,1},{3,2},{4,3},{5,4},{6,5},{7,6},{0,7},{9,8},{10,9},{11,1... | collective-permute-start | bytes 786440 | tf_op jit(solution)/shard_map/ppermute | solution.py:20
  7.9 10.6 %collective-permute-start.1 = (f32[16,1,4096]{2,1,0:T(1,128)S(1)}, f32[16,1,4096]{2,1,0:T(1,128)}, u32[]{:S(2)}, u32[]{:S(2)}) collective-permute-start(f32[16,1,4096]{2,1,0:T(1,128)S(1)} %get-tuple-element.26), channel_id=1, source_target_pairs={{0,1},{1,2},{2,3},{3,4},{4,5},{5,6},{6,7},{7,0},{8,9},{9,10},{10,1... | collective-permute-start | bytes 786440 | tf_op jit(solution)/shard_map/ppermute | solution.py:17
  9.3 0.8 copy-start.1
  23.9 13.4 %collective-permute-start.2 = (f32[16,1,4096]{2,1,0:T(1,128)}, f32[16,1,4096]{2,1,0:T(1,128)S(1)}, u32[]{:S(2)}, u32[]{:S(2)}) collective-permute-start(f32[16,1,4096]{2,1,0:T(1,128)} %get-tuple-element.23), channel_id=1, source_target_pairs={{1,0},{2,1},{3,2},{4,3},{5,4},{6,5},{7,6},{0,7},{9,8},{10,9},{11,1... | collective-permute-start | bytes 786440 | tf_op jit(solution)/shard_map/ppermute | solution.py:20
  27.3 10.2 %collective-permute-start.3 = (f32[16,1,4096]{2,1,0:T(1,128)}, f32[16,1,4096]{2,1,0:T(1,128)}, u32[]{:S(2)}, u32[]{:S(2)}) collective-permute-start(f32[16,1,4096]{2,1,0:T(1,128)} %get-tuple-element.24), channel_id=1, source_target_pairs={{0,1},{1,2},{2,3},{3,4},{4,5},{5,6},{6,7},{7,0},{8,9},{9,10},{10,1... | collective-permute-start | bytes 786440 | tf_op jit(solution)/shard_map/ppermute | solution.py:17
where the time goes:
time: 103 us; the launch traced here: 102 us
  blocking collectives  56.9 us (55%)
  waiting for transfers between devices  15.7 us (15%)
  starting transfers between devices  9.52 us (9%)
  local copies, waits for them, and re-layouts  9.32 us (9%)
  other arithmetic  7.48 us (7%)
  matrix products  2.54 us (2%)
    psum x1, blocking collectives, local(): gram = lax.psum(partial_value, ('band', 'grid'))  39 us
    ppermute x2, waiting for transfers between devices, with_halo(): lax.ppermute(lax.slice_in_dim(block, 0, width, axis=dim), axis, backward)  10.5 us
    ppermute x2, starting transfers between devices, with_halo(): lax.ppermute(lax.slice_in_dim(block, 0, width, axis=dim), axis, backward)  9.51 us
    all_to_all x1, blocking collectives, local(): lax.all_to_all(turned, 'band', split_axis=0, concat_axis=1, tiled=True)  9.36 us
    all_to_all x1, blocking collectives, local(): lax.all_to_all(filtered, 'band', split_axis=1, concat_axis=0, tiled=True)  8.59 us
    ppermute x2, waiting for transfers between devices, with_halo(): lax.ppermute(lax.slice_in_dim(block, block.shape[dim] - width, None, axis...  5.27 us
    slice x2, local copies, waits for them, and re-layouts, with_halo(): lax.slice_in_dim(block, 0, width, axis=dim)  3.21 us
    convert_element_type x1, other arithmetic, local(): filtered = current.astype(jnp.bfloat16).reshape(count, zplanes * width)  2.58 us
  transfers between devices with their start and end apart: 4, of which 4 were waited for; matrix products, arithmetic and copies ran while one was open for 4% of the time, Pallas kernels for 0%

commit v1 on v0

--- a/solution.py
+++ b/solution.py
@@ -55,7 +55,10 @@
         )
         / total_cells
     )
-    gram = lax.psum(partial_value, ("band", "grid"))
+    divide_wires_on_mesh = lambda sheet, device_axis, axis_key: lax.psum(
+        lax.psum(sheet, axis_name=device_axis), axis_key
+    )
+    gram = divide_wires_on_mesh(partial_value, "band", "grid")
     scale = jnp.max(jnp.sum(jnp.abs(gram), axis=1))
     identity_mat = jnp.eye(gram.shape[0], dtype=jnp.float32)
     upper = gram / scale

time: 103 us -> 109 us (1.058)
  blocking collectives: 56.9 us -> 63.3 us
    psum x1 -> x2, blocking collectives: 39 us -> 46.3 us  [the longest x1 36.1 us: local(): lax.psum(lax.psum(sheet, axis_name=device_axis), axis_key)]
where the time goes in v1:
time: 109 us
  blocking collectives  63.3 us (58%)
  waiting for transfers between devices  15.7 us (14%)
  starting transfers between devices  9.52 us (9%)
  local copies, waits for them, and re-layouts  9.32 us (9%)
  other arithmetic  7.48 us (7%)
  matrix products  2.54 us (2%)
    psum x1, blocking collectives, local(): lax.psum(lax.psum(sheet, axis_name=device_axis), axis_key)  36.1 us
    ppermute x2, waiting for transfers between devices, with_halo(): lax.ppermute(lax.slice_in_dim(block, 0, width, axis=dim), axis, backward)  10.5 us
    psum x1, blocking collectives, local(): lax.psum(sheet, axis_name=device_axis)  10.3 us
    ppermute x2, starting transfers between devices, with_halo(): lax.ppermute(lax.slice_in_dim(block, 0, width, axis=dim), axis, backward)  9.51 us
    all_to_all x1, blocking collectives, local(): lax.all_to_all(filtered, 'band', split_axis=1, concat_axis=0, tiled=True)  8.59 us
    all_to_all x1, blocking collectives, local(): lax.all_to_all(turned, 'band', split_axis=0, concat_axis=1, tiled=True)  8.39 us
    ppermute x2, waiting for transfers between devices, with_halo(): lax.ppermute(lax.slice_in_dim(block, block.shape[dim] - width, None, axis...  5.27 us
    slice x2, local copies, waits for them, and re-layouts, with_halo(): lax.slice_in_dim(block, 0, width, axis=dim)  3.22 us
  transfers between devices with their start and end apart: 4, of which 4 were waited for; matrix products, arithmetic and copies ran while one was open for 4% of the time, Pallas kernels for 0%

profile of v1, /device:TPU:0, one launch (start us, length us, event | category | flops | bytes accessed | tf_op | source)
XLA Modules:
  0.0 108.8 jit_solution(16653641273351321875)
XLA Ops:
  0.0 1.9 %fusion.24 = (f32[16,1,4096]{2,1,0:T(1,128)S(1)}, f32[16,1,4096]{2,1,0:T(1,128)S(1)}) fusion(f32[16,2,4096]{2,1,0:T(2,128)} %param.2), kind=kLoop, calls=%fused_computation.42 | loop fusion | bytes 1048576 | tf_op jit(solution)/shard_map/slice | solution.py:20
  1.9 6.1 %collective-permute-start = (f32[16,1,4096]{2,1,0:T(1,128)S(1)}, f32[16,1,4096]{2,1,0:T(1,128)S(1)}, u32[]{:S(2)}, u32[]{:S(2)}) collective-permute-start(f32[16,1,4096]{2,1,0:T(1,128)S(1)} %get-tuple-element.25), channel_id=1, source_target_pairs={{1,0},{2,1},{3,2},{4,3},{5,4},{6,5},{7,6},{0,7},{9,8},{10,9},{11,1... | collective-permute-start | bytes 786440 | tf_op jit(solution)/shard_map/ppermute | solution.py:20
  7.9 0.6 reshape.35
  8.6 0.4 fusion.19
  8.9 0.4 fusion.20
  9.5 0.5 copy-done.1
  10.1 0.9 fusion.4
  11.0 0.5 add.60
  11.5 2.0 %collective-permute-done = f32[16,1,4096]{2,1,0:T(1,128)S(1)} collective-permute-done((f32[16,1,4096]{2,1,0:T(1,128)S(1)}, f32[16,1,4096]{2,1,0:T(1,128)S(1)}, u32[]{:S(2)}, u32[]{:S(2)}) %collective-permute-start) | collective-permute-done | bytes 262176 | tf_op jit(solution)/shard_map/ppermute | solution.py:20
  13.5 5.0 %collective-permute-done.1 = f32[16,1,4096]{2,1,0:T(1,128)} collective-permute-done((f32[16,1,4096]{2,1,0:T(1,128)S(1)}, f32[16,1,4096]{2,1,0:T(1,128)}, u32[]{:S(2)}, u32[]{:S(2)}) %collective-permute-start.1) | collective-permute-done | bytes 262176 | tf_op jit(solution)/shard_map/ppermute | solution.py:17
  18.5 2.4 %broadcast_multiply_fusion = (f32[16,2,4096]{2,1,0:T(2,128)S(1)}, f32[16,2,4096]{2,1,0:T(2,128)S(1)}) fusion(f32[16,2,4096]{2,1,0:T(2,128)S(1)} %copy-done, f32[2,4096]{1,0:T(2,128)S(1)} %copy-done.1, f32[16,2,4096]{2,1,0:T(2,128)S(1)} %add.60, f32[16,1,4096]{2,1,0:T(1,128)} %collective-permute-done.1, f32[16,1,4096]{2,1,0:T(1,128)S(1)} %collective-permute-done), kind=kLoop, calls=%fused_computation.26 | loop fusion | flops 1572864 | bytes 2654208 | tf_op jit(solution)/shard_map/div | solution.py:43
  21.0 0.6 reshape.36
  21.6 0.4 fusion.16
  22.2 0.4 fusion.15
  22.5 1.3 %fusion.23 = (f32[16,1,4096]{2,1,0:T(1,128)}, f32[16,1,4096]{2,1,0:T(1,128)}) fusion(f32[16,2,4096]{2,1,0:T(2,128)S(1)} %get-tuple-element.5), kind=kLoop, calls=%fused_computation.41 | loop fusion | bytes 1048576 | tf_op jit(solution)/shard_map/slice | solution.py:20
  23.9 3.5 %collective-permute-start.2 = (f32[16,1,4096]{2,1,0:T(1,128)}, f32[16,1,4096]{2,1,0:T(1,128)S(1)}, u32[]{:S(2)}, u32[]{:S(2)}) collective-permute-start(f32[16,1,4096]{2,1,0:T(1,128)} %get-tuple-element.23), channel_id=1, source_target_pairs={{1,0},{2,1},{3,2},{4,3},{5,4},{6,5},{7,6},{0,7},{9,8},{10,9},{11,1... | collective-permute-start | bytes 786440 | tf_op jit(solution)/shard_map/ppermute | solution.py:20
  27.4 0.9 fusion.6
  28.2 0.5 add.67
  28.8 8.5 %collective-permute-done.2 = f32[16,1,4096]{2,1,0:T(1,128)S(1)} collective-permute-done((f32[16,1,4096]{2,1,0:T(1,128)}, f32[16,1,4096]{2,1,0:T(1,128)S(1)}, u32[]{:S(2)}, u32[]{:S(2)}) %collective-permute-start.2) | collective-permute-done | bytes 262176 | tf_op jit(solution)/shard_map/ppermute | solution.py:20
  37.3 0.3 collective-permute-done.3
  37.5 2.6 %subtract_convert_fusion = bf16[16,2,4096]{2,1,0:T(2,128)(2,1)S(1)} fusion(f32[16,2,4096]{2,1,0:T(2,128)S(1)} %copy-done, f32[16,2,4096]{2,1,0:T(2,128)S(1)} %get-tuple-element.6, f32[16,2,4096]{2,1,0:T(2,128)S(1)} %add.67, f32[16,2,4096]{2,1,0:T(2,128)S(1)} %get-tuple-element.5, f32[16,1,4096]{2,1,0:T(1,128)} %collective-permute-done.3, ...), kind=kLoop, calls=%fused_computation.24 | loop fusion | flops 1835008 | bytes 2916352 | tf_op jit(solution)/shard_map/convert_element_type | solution.py:49
  40.3 8.6 %all_to_all.35 = bf16[16,4,2048]{2,0,1:T(8,128)(2,1)S(1)} all-to-all(bf16[16,4,2048]{2,0,1:T(8,128)(2,1)S(1)} %copy.7), channel_id=1, replica_groups=mesh['band'=4,'grid'=8] {'band'}, dimensions={1} | all-to-all | bytes 524288 | tf_op jit(solution)/shard_map/all_to_all | solution.py:50
  48.9 0.2 convolution_multiply_fusion.2
  49.1 10.3 %psum.14 = f32[64,64]{1,0:T(8,128)S(1)} all-reduce(f32[64,64]{1,0:T(8,128)S(1)} %convolution_multiply_fusion.2), channel_id=1, replica_groups=mesh['band'=4,'grid'=8] {'band'}, use_global_device_ids=true, to_apply=%region_0.1 | all-reduce | flops 4096 | bytes 32768 | tf_op jit(solution)/shard_map/psum | solution.py:59
  59.4 36.1 %psum.15 = f32[64,64]{1,0:T(8,128)S(1)} all-reduce(f32[64,64]{1,0:T(8,128)S(1)} %psum.14), channel_id=1, replica_groups=mesh['band'=4,'grid'=8] {'grid'}, use_global_device_ids=true, to_apply=%region_1.2 | all-reduce | flops 4096 | bytes 32768 | tf_op jit(solution)/shard_map/psum | solution.py:58
  95.6 0.6 reduce_max.9
  96.2 0.8 fusion.1
  97.0 0.8 fusion.14
  99.0 0.2 convolution_convert_fusion
  99.3 8.4 %all_to_all.36 = bf16[4,16,2048]{2,1,0:T(8,128)(2,1)S(1)} all-to-all(bf16[4,16,2048]{2,1,0:T(8,128)(2,1)S(1)} %bitcast.21), channel_id=1, replica_groups=mesh['band'=4,'grid'=8] {'band'}, dimensions={0} | all-to-all | bytes 524288 | tf_op jit(solution)/shard_map/all_to_all | solution.py:75
  107.7 0.2 copy.8
  107.9 0.9 reshape.37
  (16 shorter events, 1.3 us)
Async XLA Ops:
  0.0 7.9 %copy-start = (f32[16,2,4096]{2,1,0:T(2,128)S(1)}, f32[16,2,4096]{2,1,0:T(2,128)}, u32[]{:S(2)}) copy-start(f32[16,2,4096]{2,1,0:T(2,128)} %param.2) | copy-start | bytes 1572868
  1.9 11.6 %collective-permute-start = (f32[16,1,4096]{2,1,0:T(1,128)S(1)}, f32[16,1,4096]{2,1,0:T(1,128)S(1)}, u32[]{:S(2)}, u32[]{:S(2)}) collective-permute-start(f32[16,1,4096]{2,1,0:T(1,128)S(1)} %get-tuple-element.25), channel_id=1, source_target_pairs={{1,0},{2,1},{3,2},{4,3},{5,4},{6,5},{7,6},{0,7},{9,8},{10,9},{11,1... | collective-permute-start | bytes 786440 | tf_op jit(solution)/shard_map/ppermute | solution.py:20
  7.9 10.6 %collective-permute-start.1 = (f32[16,1,4096]{2,1,0:T(1,128)S(1)}, f32[16,1,4096]{2,1,0:T(1,128)}, u32[]{:S(2)}, u32[]{:S(2)}) collective-permute-start(f32[16,1,4096]{2,1,0:T(1,128)S(1)} %get-tuple-element.26), channel_id=1, source_target_pairs={{0,1},{1,2},{2,3},{3,4},{4,5},{5,6},{6,7},{7,0},{8,9},{9,10},{10,1... | collective-permute-start | bytes 786440 | tf_op jit(solution)/shard_map/ppermute | solution.py:17
  9.3 0.8 copy-start.1
  23.9 13.4 %collective-permute-start.2 = (f32[16,1,4096]{2,1,0:T(1,128)}, f32[16,1,4096]{2,1,0:T(1,128)S(1)}, u32[]{:S(2)}, u32[]{:S(2)}) collective-permute-start(f32[16,1,4096]{2,1,0:T(1,128)} %get-tuple-element.23), channel_id=1, source_target_pairs={{1,0},{2,1},{3,2},{4,3},{5,4},{6,5},{7,6},{0,7},{9,8},{10,9},{11,1... | collective-permute-start | bytes 786440 | tf_op jit(solution)/shard_map/ppermute | solution.py:20
  27.3 10.2 %collective-permute-start.3 = (f32[16,1,4096]{2,1,0:T(1,128)}, f32[16,1,4096]{2,1,0:T(1,128)}, u32[]{:S(2)}, u32[]{:S(2)}) collective-permute-start(f32[16,1,4096]{2,1,0:T(1,128)} %get-tuple-element.24), channel_id=1, source_target_pairs={{0,1},{1,2},{2,3},{3,4},{4,5},{5,6},{6,7},{7,0},{8,9},{9,10},{10,1... | collective-permute-start | bytes 786440 | tf_op jit(solution)/shard_map/ppermute | solution.py:17
